TPU v7x, 256 devices: a whole 4x4x8 slice. The times are simulated.
256 devices in a mesh: tm: 16 (over z, core), space: 16 (over x, y).
Axes of the slice: x: 4, y: 4, z: 8, core: 2. Of those that a mesh axis runs over, the one named last changes fastest.
Arguments:
- concentration: float32 [4, 16, 1024, 2048], P(None, 'tm', 'space'), may hold values from -5.5 to 5.5
- forcing: float32 [4, 16, 1024, 2048], P(None, 'tm', 'space'), may hold values from -5.5 to 5.5
- eigenbasis: bfloat16 [2048, 2048], replicated, may hold values from -0.125 to 0.125
- eigenvalues: float32 [2048], replicated, may hold values from -0.5 to -0.001, as said below
- settle_table: float32 [8], replicated, may hold values from 0.002 to 0.5, as said below
- fraction_class: int32 [4], replicated, may hold values from 0 to 7
- bed_mask: int32 [1024, 2048], P('space'), may hold values 0 or 1
Outputs:
- updated: float32 [4, 16, 1024, 2048], P(None, 'tm', 'space')
Inputs may be any that keep to these rules, and one draw needn't show every extreme that they name: `fraction_class`: index into settle_table. `bed_mask`: 1 marks a bed cell. `eigenvalues`: negative. `settle_table`: positive.
All inputs are finite; a program needn't handle non-finite values. No bound on the sum of `bed_mask` on one device may be relied on, other than what follows from the above.
Results may differ from a plain program's by a relative error of at most 0.0055.
Values may be sent and summed in bfloat16 or wider, within the bound.
A program may use at most 64 MiB of HBM per device.

v0:
```python
import math
import jax
import jax.numpy as jnp
from jax import lax
from jax.sharding import PartitionSpec as P

CIRCULANT_ALPHA = 0.5
VERTICAL_DIFFUSION = 0.06
DEPOSITION = 0.1


def extended(block, sides, width):
    for axis, dim in sides:
        count = lax.axis_size(axis)
        forward = [(i, i + 1) for i in range(count - 1)]
        backward = [(target, source) for source, target in forward]
        low = lax.ppermute(
            lax.slice_in_dim(block, block.shape[dim] - width, None, axis=dim), axis, forward
        )
        high = lax.ppermute(lax.slice_in_dim(block, 0, width, axis=dim), axis, backward)
        block = jnp.concatenate([low, block, high], axis=dim)
    return block


def from_behind(value, axis, steps):
    count = lax.axis_size(axis)
    initial, last = (max(0, -steps), min(count, count - steps))
    return lax.ppermute(value, axis, [(source, source + steps) for source in range(initial, last)])


def twiddles(first_index, second_index, length):
    products = first_index[:, None] * second_index[None, :] % length
    angle_grid = 2.0 * math.pi / length * products.astype(jnp.float32)
    return (jnp.cos(angle_grid), jnp.sin(angle_grid))


def apply_table(table, values):
    return jnp.einsum(
        "kn,fnrx->fkrx", table, values.astype(jnp.float32), precision=lax.Precision.HIGHEST
    )


def to_space(modal, eigenbasis):
    return lax.dot_general(
        modal, eigenbasis, (((1,), (1,)), ((), ())), preferred_element_type=jnp.float32
    )


def solve_shifted(
    real_part, imag_part, freq_index, length, decay_ratio, eigenbasis, eigenvalues, diagonal
):
    layout = real_part.shape
    columns = layout[-1]
    stacked = (
        jnp.concatenate([real_part, imag_part], axis=0).astype(jnp.bfloat16).reshape(-1, columns)
    )
    modal = jnp.dot(stacked, eigenbasis, preferred_element_type=jnp.float32).reshape((2,) + layout)
    angles = 2.0 * math.pi / length * freq_index.astype(jnp.float32)
    shift_real = (
        (1.0 - decay_ratio * jnp.cos(angles))[None, :, None, None]
        - eigenvalues[None, None, None, :]
        + diagonal[:, None, None, None]
    )
    shift_imag = (decay_ratio * jnp.sin(angles))[None, :, None, None]
    magnitude = shift_real * shift_real + shift_imag * shift_imag
    scaled_real = (modal[0] * shift_real + modal[1] * shift_imag) / magnitude
    scaled_imag = (modal[1] * shift_real - modal[0] * shift_imag) / magnitude
    scaled = (
        jnp.concatenate([scaled_real, scaled_imag], axis=0)
        .astype(jnp.bfloat16)
        .reshape(-1, columns)
    )
    back = to_space(scaled, eigenbasis).astype(jnp.bfloat16).reshape((2,) + layout)
    return (back[0], back[1])


def on_device(
    concentration, forcing, eigenbasis, eigenvalues, settle_table, fraction_class, bed_mask
):
    fractions, slices, row_count, columns = concentration.shape
    tm_devices = lax.axis_size("tm")
    length = slices * tm_devices
    classes = settle_table.shape[0]
    onehot = (fraction_class[:, None] == jnp.arange(classes, dtype=jnp.int32)[None, :]).astype(
        jnp.float32
    )
    settling = jnp.sum(onehot * settle_table[None, :], axis=1)
    diagonal = 2.0 * VERTICAL_DIFFUSION + settling
    decay_ratio = CIRCULANT_ALPHA ** (1.0 / length)
    first_slice = lax.axis_index("tm") * slices
    slice_index = first_slice + jnp.arange(slices, dtype=jnp.int32)
    slice_times = slice_index.astype(jnp.float32)
    scale_up = decay_ratio**slice_times
    scale_down = decay_ratio ** (-slice_times)
    bed_cells = bed_mask.astype(jnp.float32)
    padded = extended(concentration, (("space", 2),), 1)
    upper_row = padded[:, :, :-2]
    lower_row = padded[:, :, 2:]
    vertical = (
        VERTICAL_DIFFUSION * (lower_row - 2.0 * concentration + upper_row)
        + settling[:, None, None, None] * (upper_row - concentration)
        - DEPOSITION * bed_cells[None, None] * concentration
    )
    coupled = (
        jnp.dot(
            concentration.astype(jnp.bfloat16).reshape(-1, columns),
            eigenbasis,
            preferred_element_type=jnp.float32,
        )
        * eigenvalues[None, :]
    ).astype(jnp.bfloat16)
    along_x = to_space(coupled, eigenbasis).reshape(concentration.shape)
    last_slice = from_behind(concentration, "tm", 1)
    earlier = jnp.concatenate([last_slice, concentration[:, : slices - 1]], axis=1)
    residual = forcing - (concentration - along_x - vertical - earlier)
    scaled = (scale_up[None, :, None, None] * residual).astype(jnp.bfloat16)
    by_rows = lax.all_to_all(scaled, "tm", split_axis=2, concat_axis=1, tiled=True)
    all_index = jnp.arange(length, dtype=jnp.int32)
    cosine_table, sine_table = twiddles(all_index, all_index, length)
    real_part = apply_table(cosine_table, by_rows)
    imag_part = -apply_table(sine_table, by_rows)
    back_real, back_imag = solve_shifted(
        real_part, imag_part, all_index, length, decay_ratio, eigenbasis, eigenvalues, diagonal
    )
    relaxed_rows = (
        apply_table(cosine_table, back_real) - apply_table(sine_table, back_imag)
    ) / length
    relaxed = lax.all_to_all(relaxed_rows, "tm", split_axis=1, concat_axis=2, tiled=True)
    return concentration + scale_down[None, :, None, None] * relaxed


def solution(mesh):
    return jax.shard_map(
        on_device,
        mesh=mesh,
        in_specs=(
            P(None, "tm", "space", None),
            P(None, "tm", "space", None),
            P(),
            P(),
            P(),
            P(),
            P("space", None),
        ),
        out_specs=P(None, "tm", "space", None),
        check_vma=False,
    )
```

profile of v0, /device:TPU:1, one launch (start us, length us, event | category | flops | bytes accessed | tf_op | source)
XLA Modules:
  0.0 189.0 jit_solution(3372452159803485570)
XLA Ops:
  0.0 5.0 %collective-permute-start.2 = (f32[4,1,64,2048]{3,2,1,0:T(8,128)}, f32[4,1,64,2048]{3,2,1,0:T(8,128)}, u32[]{:S(2)}, u32[]{:S(2)}) collective-permute-start(f32[4,1,64,2048]{3,2,1,0:T(8,128)} %param.7), channel_id=1, source_target_pairs={{0,16},{16,32},{32,48},{48,64},{64,80},{80,96},{96,112},{112,128},... | collective-permute-start | bytes 6291464 | tf_op jit(solution)/shard_map/ppermute | solution.py:28
  7.5 4.0 %collective-permute-start.1 = (f32[4,1,1,2048]{3,2,1,0:T(1,128)S(1)}, f32[4,1,1,2048]{3,2,1,0:T(1,128)S(1)}, u32[]{:S(2)}, u32[]{:S(2)}) collective-permute-start(f32[4,1,1,2048]{3,2,1,0:T(1,128)S(1)} %get-tuple-element.12), channel_id=1, source_target_pairs={{0,1},{1,2},{2,3},{3,4},{4,5},{5,6},{6,7},{7,8},{8,9},{9,10},{10,1... | collective-permute-start | bytes 98312 | tf_op jit(solution)/shard_map/ppermute | solution.py:17
  11.4 2.7 %convert_element_type.63 = bf16[4,1,64,2048]{3,2,1,0:T(8,128)(2,1)} convert(f32[4,1,64,2048]{3,2,1,0:T(8,128)} %param.7) | non-fusion elementwise | flops 524288 | bytes 3145728 | tf_op jit(solution)/shard_map/convert_element_type | solution.py:106
  14.3 12.0 %fusion.25 = f32[256,2048]{1,0:T(8,128)} fusion(bf16[2048,2048]{1,0:T(8,128)(2,1)} %param.9, bf16[256,2048]{1,0:T(8,128)(2,1)} %bitcast.37, f32[2048]{0:T(1024)S(1)} %copy-done.4), kind=kOutput, calls=%fused_computation.38 | convolution fusion | flops 4296015872 | bytes 11542528 | tf_op jit(solution)/shard_map/dot_general | solution.py:44
  28.3 3.5 %fusion.15 = bf16[4,1,64,2048]{3,2,1,0:T(8,128)(2,1)S(1)} fusion(f32[4,1,64,2048]{3,2,1,0:T(8,128)} %param.8, f32[4,1,64,2048]{3,2,1,0:T(8,128)} %collective-permute-done.2, f32[4,1,64,2048]{3,2,1,0:T(8,128)S(1)} %copy-done, f32[4,1,1,2048]{3,2,1,0:T(1,128)S(1)} %collective-permute-done.1, f32[4,1,1,2048]{3,2,1,0:T(1,128)S(1)} %collective-permute-done, ...), kind=kLoop, calls=%fused_computation.21 | loop fusion | flops 8912896 | bytes 10027028 | tf_op jit(solution)/shard_map/convert_element_type | solution.py:116
  33.7 10.6 %all-to-all-start = ((bf16[4,1,64,2048]{3,0,1,2:T(4,128)(2,1)}), bf16[4,1,64,2048]{3,0,1,2:T(4,128)(2,1)S(1)}, u32[]{:S(2)}, u32[]{:S(2)}) async-start(bf16[4,1,64,2048]{3,0,1,2:T(4,128)(2,1)} %copy.66), calls=%async_computation | async-start | bytes 2097152 | tf_op jit(solution)/shard_map/all_to_all | solution.py:117
  45.7 26.6 %all-to-all-done = bf16[4,1,64,2048]{3,0,1,2:T(4,128)(2,1)S(1)} async-done(((bf16[4,1,64,2048]{3,0,1,2:T(4,128)(2,1)}), bf16[4,1,64,2048]{3,0,1,2:T(4,128)(2,1)S(1)}, u32[]{:S(2)}, u32[]{:S(2)}) %all-to-all-start) | async-done | bytes 1048608 | tf_op jit(solution)/shard_map/all_to_all | solution.py:117
  75.8 3.0 %copy.69 = bf16[8,16,4,2048]{3,2,1,0:T(4,128)(2,1)} copy(bf16[8,16,4,2048]{3,1,2,0:T(8,128)(2,1)S(1)} %pad_maximum_fusion.2) | data formatting | bytes 4194304 | tf_op jit(solution)/shard_map/concatenate | solution.py:55
  78.7 4.0 %convert_element_type.68 = bf16[512,2048]{1,0:T(8,128)(2,1)} reshape(bf16[8,16,4,2048]{3,2,1,0:T(4,128)(2,1)} %copy.69) | data formatting | bytes 4194304 | tf_op jit(solution)/shard_map/convert_element_type | solution.py:55
  82.7 7.6 %fusion.62 = f32[512,2048]{1,0:T(8,128)S(1)} fusion(bf16[512,2048]{1,0:T(8,128)(2,1)} %convert_element_type.68, bf16[2048,2048]{1,0:T(8,128)(2,1)} %param.9), kind=kOutput, calls=%fused_computation.84 | convolution fusion | flops 4294967296 | bytes 14680064 | tf_op jit(solution)/shard_map/dot_general | solution.py:57
  90.3 2.3 %fusion.59 = (f32[256,2048]{1,0:T(8,128)}, f32[256,2048]{1,0:T(8,128)}) fusion(f32[512,2048]{1,0:T(8,128)S(1)} %fusion.62), kind=kLoop, calls=%fused_computation.81 | loop fusion | bytes 8388608 | tf_op jit(solution)/shard_map/slice | solution.py:66
  92.6 2.9 %squeeze.14 = f32[4,16,4,2048]{3,2,1,0:T(4,128)} reshape(f32[256,2048]{1,0:T(8,128)} %get-tuple-element.8) | data formatting | bytes 4194304 | tf_op jit(solution)/shard_map/squeeze | solution.py:66
  95.4 2.9 %squeeze.15 = f32[4,16,4,2048]{3,2,1,0:T(4,128)} reshape(f32[256,2048]{1,0:T(8,128)} %get-tuple-element.7) | data formatting | bytes 4194304 | tf_op jit(solution)/shard_map/squeeze | solution.py:66
  98.4 3.3 %fusion.18 = (bf16[4,16,4,2048]{3,2,1,0:T(4,128)(2,1)S(1)}, bf16[4,16,4,2048]{3,2,1,0:T(4,128)(2,1)S(1)}) fusion(f32[4,16,4,2048]{3,2,1,0:T(4,128)} %squeeze.15, f32[4,16,4,2048]{3,2,1,0:T(4,128)} %squeeze.14, f32[4,16,2048]{2,1,0:T(8,128)S(1)} %copy-done.2, f32[16]{0:T(128)S(1)} %sine_multiply_fusion, f32[4,16,2048]{2,1,0:T(8,128)S(1)} %copy-done.1), kind=kLoop, calls=%fused_computation.31 | loop fusion | flops 5242880 | bytes 7340096 | tf_op jit(solution)/shard_map/convert
  101.7 2.7 %pad_maximum_fusion.3 = bf16[8,16,4,2048]{3,2,1,0:T(4,128)(2,1)} fusion(bf16[4,16,4,2048]{3,2,1,0:T(4,128)(2,1)S(1)} %get-tuple-element.6, bf16[4,16,4,2048]{3,2,1,0:T(4,128)(2,1)S(1)} %get-tuple-element.5), kind=kLoop, calls=%fused_computation.26 | loop fusion | flops 1048576 | bytes 4194304 | tf_op jit(solution)/shard_map/concatenate | solution.py:69
  104.4 4.0 %convert_element_type.70 = bf16[512,2048]{1,0:T(8,128)(2,1)} reshape(bf16[8,16,4,2048]{3,2,1,0:T(4,128)(2,1)} %pad_maximum_fusion.3) | data formatting | bytes 4194304 | tf_op jit(solution)/shard_map/convert_element_type | solution.py:70
  108.3 8.5 %convolution_convert_fusion = bf16[512,2048]{1,0:T(8,128)(2,1)S(1)} fusion(bf16[512,2048]{1,0:T(8,128)(2,1)} %convert_element_type.70, bf16[2048,2048]{1,0:T(8,128)(2,1)} %param.9), kind=kOutput, calls=%fused_computation | convolution fusion | flops 4296015872 | bytes 12582912 | tf_op jit(solution)/shard_map/dot_general | solution.py:44
  119.8 2.7 %fusion.21 = f32[4,4,2048,16]{2,3,1,0:T(8,128)} fusion(bf16[4,16,4,2048]{3,2,1,0:T(4,128)(2,1)S(1)} %squeeze.16), kind=kOutput, calls=%fused_computation.34 | convolution fusion | flops 100666880 | bytes 3145728 | tf_op jit(solution)/shard_map/kn,fnrx->fkrx/dot_general | solution.py:38
  123.9 3.1 %fusion.1 = f32[4,16,4,2048]{3,1,2,0:T(8,128)S(1)} fusion(f32[4,4,2048,16]{2,3,1,0:T(8,128)} %fusion.21, bf16[4,16,4,2048]{3,2,1,0:T(4,128)(2,1)S(1)} %squeeze.17), kind=kOutput, calls=%fused_computation.5 | convolution fusion | flops 101715456 | bytes 5242880 | tf_op jit(solution)/shard_map/kn,fnrx->fkrx/dot_general | solution.py:38
  127.0 2.7 %copy.72 = f32[4,16,4,2048]{3,2,0,1:T(4,128)} copy(f32[4,16,4,2048]{3,1,2,0:T(8,128)S(1)} %fusion.1) | data formatting | bytes 4194304 | tf_op jit(solution)/shard_map/div | solution.py:125
  129.7 4.6 %all-to-all-start.1 = ((f32[4,16,4,2048]{3,2,0,1:T(4,128)}), f32[4,16,4,2048]{3,2,0,1:T(4,128)}, u32[]{:S(2)}, u32[]{:S(2)}) async-start(f32[4,16,4,2048]{3,2,0,1:T(4,128)} %copy.72), calls=%async_computation.1 | async-start | bytes 4194304 | tf_op jit(solution)/shard_map/all_to_all | solution.py:128
  134.3 47.9 %all-to-all-done.1 = f32[4,16,4,2048]{3,2,0,1:T(4,128)} async-done(((f32[4,16,4,2048]{3,2,0,1:T(4,128)}), f32[4,16,4,2048]{3,2,0,1:T(4,128)}, u32[]{:S(2)}, u32[]{:S(2)}) %all-to-all-start.1) | async-done | bytes 2097184 | tf_op jit(solution)/shard_map/all_to_all | solution.py:128
  182.2 2.8 %copy_multiply_fusion = f32[4,16,4,2048]{3,1,2,0:T(8,128)S(1)} fusion(f32[4,16,4,2048]{3,2,0,1:T(4,128)} %all-to-all-done.1, f32[]{:T(128)S(6)} %pow.8), kind=kLoop, calls=%fused_computation.28 | loop fusion | flops 524288 | bytes 4194308 | tf_op jit(solution)/shard_map/mul | solution.py:129
  186.4 2.6 %copy_add_fusion = f32[4,1,64,2048]{3,2,1,0:T(8,128)} fusion(f32[4,1,64,2048]{3,2,1,0:T(8,128)S(1)} %copy-done, f32[4,1,64,2048]{3,0,2,1:T(4,128)S(1)} %bitcast.35), kind=kLoop, calls=%fused_computation.27 | loop fusion | flops 524288 | bytes 6291456 | tf_op jit(solution)/shard_map/add | solution.py:129
  (35 shorter events, 16.7 us)
Async XLA Ops:
  0.0 14.2 %copy-start.3 = (s32[64,2048]{1,0:T(8,128)S(1)}, s32[64,2048]{1,0:T(8,128)}, u32[]{:S(2)}) copy-start(s32[64,2048]{1,0:T(8,128)} %param.13) | copy-start | bytes 1572868
  0.0 28.3 %collective-permute-start.2 = (f32[4,1,64,2048]{3,2,1,0:T(8,128)}, f32[4,1,64,2048]{3,2,1,0:T(8,128)}, u32[]{:S(2)}, u32[]{:S(2)}) collective-permute-start(f32[4,1,64,2048]{3,2,1,0:T(8,128)} %param.7), channel_id=1, source_target_pairs={{0,16},{16,32},{32,48},{48,64},{64,80},{80,96},{96,112},{112,128},... | collective-permute-start | bytes 6291464 | tf_op jit(solution)/shard_map/ppermute | solution.py:28
  6.1 20.4 %collective-permute-start = (f32[4,1,1,2048]{3,2,1,0:T(1,128)S(1)}, f32[4,1,1,2048]{3,2,1,0:T(1,128)S(1)}, u32[]{:S(2)}, u32[]{:S(2)}) collective-permute-start(f32[4,1,1,2048]{3,2,1,0:T(1,128)S(1)} %get-tuple-element.11), channel_id=1, source_target_pairs={{1,0},{2,1},{3,2},{4,3},{5,4},{6,5},{7,6},{8,7},{9,8},{10,9},{11,1... | collective-permute-start | bytes 98312 | tf_op jit(solution)/shard_map/ppermute | solution.py:20
  7.4 6.8 %copy-start.4 = (f32[2048]{0:T(1024)S(1)}, f32[2048]{0:T(1024)}, u32[]{:S(2)}) copy-start(f32[2048]{0:T(1024)} %param.10) | copy-start | bytes 24580
  7.5 19.1 %collective-permute-start.1 = (f32[4,1,1,2048]{3,2,1,0:T(1,128)S(1)}, f32[4,1,1,2048]{3,2,1,0:T(1,128)S(1)}, u32[]{:S(2)}, u32[]{:S(2)}) collective-permute-start(f32[4,1,1,2048]{3,2,1,0:T(1,128)S(1)} %get-tuple-element.12), channel_id=1, source_target_pairs={{0,1},{1,2},{2,3},{3,4},{4,5},{5,6},{6,7},{7,8},{8,9},{9,10},{10,1... | collective-permute-start | bytes 98312 | tf_op jit(solution)/shard_map/ppermute | solution.py:17
  14.2 12.1 %copy-start.5 = (f32[8]{0:T(128)S(1)}, f32[8]{0:T(128)}, u32[]{:S(2)}) copy-start(f32[8]{0:T(128)} %param.11) | copy-start | bytes 100
  14.2 12.1 %copy-start.6 = (s32[4]{0:T(128)S(1)}, s32[4]{0:T(128)}, u32[]{:S(2)}) copy-start(s32[4]{0:T(128)} %param.12) | copy-start | bytes 52
  14.2 14.1 %copy-start = (f32[4,1,64,2048]{3,2,1,0:T(8,128)S(1)}, f32[4,1,64,2048]{3,2,1,0:T(8,128)}, u32[]{:S(2)}) copy-start(f32[4,1,64,2048]{3,2,1,0:T(8,128)} %param.7) | copy-start | bytes 6291460
  33.7 38.6 %all-to-all-start = ((bf16[4,1,64,2048]{3,0,1,2:T(4,128)(2,1)}), bf16[4,1,64,2048]{3,0,1,2:T(4,128)(2,1)S(1)}, u32[]{:S(2)}, u32[]{:S(2)}) async-start(bf16[4,1,64,2048]{3,0,1,2:T(4,128)(2,1)} %copy.66), calls=%async_computation | async-start | bytes 2097152 | tf_op jit(solution)/shard_map/all_to_all | solution.py:117
  95.4 3.0 %copy-start.1 = (f32[4,16,2048]{2,1,0:T(8,128)S(1)}, f32[4,16,2048]{2,1,0:T(8,128)}, u32[]{:S(2)}) copy-start(f32[4,16,2048]{2,1,0:T(8,128)} %get-tuple-element.13) | copy-start | bytes 1572868
  95.4 3.0 %copy-start.2 = (f32[4,16,2048]{2,1,0:T(8,128)S(1)}, f32[4,16,2048]{2,1,0:T(8,128)}, u32[]{:S(2)}) copy-start(f32[4,16,2048]{2,1,0:T(8,128)} %get-tuple-element.14) | copy-start | bytes 1572868
  129.7 52.5 %all-to-all-start.1 = ((f32[4,16,4,2048]{3,2,0,1:T(4,128)}), f32[4,16,4,2048]{3,2,0,1:T(4,128)}, u32[]{:S(2)}, u32[]{:S(2)}) async-start(f32[4,16,4,2048]{3,2,0,1:T(4,128)} %copy.72), calls=%async_computation.1 | async-start | bytes 4194304 | tf_op jit(solution)/shard_map/all_to_all | solution.py:128
where the time goes:
time: 190 us; the launch traced here: 189 us
  waiting for transfers between devices  76.3 us (40%)
  matrix products  37.2 us (20%)
  local copies, waits for them, and re-layouts  30.3 us (16%)
  starting transfers between devices  25.6 us (13%)
  other arithmetic  19.5 us (10%)
    all_to_all x1, waiting for transfers between devices, on_device(): lax.all_to_all(relaxed_rows, 'tm', split_axis=1, concat_axis=2, tiled=True)  47.9 us
    all_to_all x1, waiting for transfers between devices, on_device(): lax.all_to_all(scaled, 'tm', split_axis=2, concat_axis=1, tiled=True)  26.6 us
    dot_general x2, matrix products, to_space(): lax.dot_general(modal, eigenbasis, (((1,), (1,)), ((), ())), preferred_el...  20.6 us
    all_to_all x1, starting transfers between devices, on_device(): lax.all_to_all(scaled, 'tm', split_axis=2, concat_axis=1, tiled=True)  10.6 us
    dot_general x4, matrix products, apply_table(): jnp.einsum('kn,fnrx->fkrx', table, values.astype(jnp.float32), precision=...  9.01 us
    dot_general x1, matrix products, solve_shifted(): jnp.dot(stacked, eigenbasis, preferred_element_type=jnp.float32)  7.56 us
    squeeze x2, local copies, waits for them, and re-layouts, solve_shifted(): scaled_real = (modal[0] * shift_real + modal[1] * shift_imag) / magnitude  5.81 us
    ppermute x1, starting transfers between devices, from_behind(): lax.ppermute(value, axis, [(source, source + steps) for source in range(i...  5.05 us
  transfers between devices with their start and end apart: 5, of which 3 were waited for; matrix products, arithmetic and copies ran while one was open for 9% of the time, Pallas kernels for 0%

commit v1 on v0

--- a/solution.py
+++ b/solution.py
@@ -114,7 +114,10 @@
     earlier = jnp.concatenate([last_slice, concentration[:, : slices - 1]], axis=1)
     residual = forcing - (concentration - along_x - vertical - earlier)
     scaled = (scale_up[None, :, None, None] * residual).astype(jnp.bfloat16)
-    by_rows = lax.all_to_all(scaled, "tm", split_axis=2, concat_axis=1, tiled=True)
+    by_rows = jnp.concatenate(
+        lax.all_to_all(jnp.stack(jnp.split(scaled, lax.axis_size("tm"), axis=2)), "tm", 0, 0),
+        axis=1,
+    )
     all_index = jnp.arange(length, dtype=jnp.int32)
     cosine_table, sine_table = twiddles(all_index, all_index, length)
     real_part = apply_table(cosine_table, by_rows)

time: 190 us -> 198 us (1.042)
  local copies, waits for them, and re-layouts: 30.3 us -> 39 us
    unnamed x14 -> x29, local copies, waits for them, and re-layouts: 0.04 us -> 9.88 us
where the time goes in v1:
time: 198 us; the launch traced here: 197 us
  waiting for transfers between devices  76.3 us (39%)
  local copies, waits for them, and re-layouts  39 us (20%)
  matrix products  36.5 us (18%)
  starting transfers between devices  25.6 us (13%)
  other arithmetic  19.5 us (10%)
    all_to_all x1, waiting for transfers between devices, on_device(): lax.all_to_all(relaxed_rows, 'tm', split_axis=1, concat_axis=2, tiled=True)  47.9 us
    all_to_all x1, waiting for transfers between devices, on_device(): lax.all_to_all(jnp.stack(jnp.split(scaled, lax.axis_size('tm'), axis=2)),...  26.6 us
    dot_general x2, matrix products, to_space(): lax.dot_general(modal, eigenbasis, (((1,), (1,)), ((), ())), preferred_el...  20.6 us
    all_to_all x1, starting transfers between devices, on_device(): lax.all_to_all(jnp.stack(jnp.split(scaled, lax.axis_size('tm'), axis=2)),...  10.6 us
    unnamed x29, local copies, waits for them, and re-layouts  9.88 us
    dot_general x4, matrix products, apply_table(): jnp.einsum('kn,fnrx->fkrx', table, values.astype(jnp.float32), precision=...  8.37 us
    dot_general x1, matrix products, solve_shifted(): jnp.dot(stacked, eigenbasis, preferred_element_type=jnp.float32)  7.56 us
    squeeze x2, local copies, waits for them, and re-layouts, solve_shifted(): scaled_real = (modal[0] * shift_real + modal[1] * shift_imag) / magnitude  5.81 us
  transfers between devices with their start and end apart: 5, of which 3 were waited for; matrix products, arithmetic and copies ran while one was open for 9% of the time, Pallas kernels for 0%

profile of v1, /device:TPU:1, one launch (start us, length us, event | category | flops | bytes accessed | tf_op | source)
XLA Modules:
  0.0 197.1 jit_solution(7681795307165745848)
XLA Ops:
  0.0 5.0 %collective-permute-start.2 = (f32[4,1,64,2048]{3,2,1,0:T(8,128)}, f32[4,1,64,2048]{3,2,1,0:T(8,128)}, u32[]{:S(2)}, u32[]{:S(2)}) collective-permute-start(f32[4,1,64,2048]{3,2,1,0:T(8,128)} %param.7), channel_id=1, source_target_pairs={{0,16},{16,32},{32,48},{48,64},{64,80},{80,96},{96,112},{112,128},... | collective-permute-start | bytes 6291464 | tf_op jit(solution)/shard_map/ppermute | solution.py:28
  7.5 4.0 %collective-permute-start.1 = (f32[4,1,1,2048]{3,2,1,0:T(1,128)S(1)}, f32[4,1,1,2048]{3,2,1,0:T(1,128)S(1)}, u32[]{:S(2)}, u32[]{:S(2)}) collective-permute-start(f32[4,1,1,2048]{3,2,1,0:T(1,128)S(1)} %get-tuple-element.12), channel_id=1, source_target_pairs={{0,1},{1,2},{2,3},{3,4},{4,5},{5,6},{6,7},{7,8},{8,9},{9,10},{10,1... | collective-permute-start | bytes 98312 | tf_op jit(solution)/shard_map/ppermute | solution.py:17
  11.4 2.7 %convert_element_type.63 = bf16[4,1,64,2048]{3,2,1,0:T(8,128)(2,1)} convert(f32[4,1,64,2048]{3,2,1,0:T(8,128)} %param.7) | non-fusion elementwise | flops 524288 | bytes 3145728 | tf_op jit(solution)/shard_map/convert_element_type | solution.py:106
  14.3 12.0 %fusion.27 = f32[256,2048]{1,0:T(8,128)} fusion(bf16[2048,2048]{1,0:T(8,128)(2,1)} %param.9, bf16[256,2048]{1,0:T(8,128)(2,1)} %bitcast.105, f32[2048]{0:T(1024)S(1)} %copy-done.4), kind=kOutput, calls=%fused_computation.40 | convolution fusion | flops 4296015872 | bytes 11542528 | tf_op jit(solution)/shard_map/dot_general | solution.py:44
  28.3 3.5 %fusion.15 = bf16[4,1,64,2048]{3,2,1,0:T(8,128)(2,1)S(1)} fusion(f32[4,1,64,2048]{3,2,1,0:T(8,128)} %param.8, f32[4,1,64,2048]{3,2,1,0:T(8,128)} %collective-permute-done.2, f32[4,1,64,2048]{3,2,1,0:T(8,128)S(1)} %copy-done, f32[4,1,1,2048]{3,2,1,0:T(1,128)S(1)} %collective-permute-done.1, f32[4,1,1,2048]{3,2,1,0:T(1,128)S(1)} %collective-permute-done, ...), kind=kLoop, calls=%fused_computation.21 | loop fusion | flops 8912896 | bytes 10027028 | tf_op jit(solution)/shard_map/convert_element_type | solution.py:116
  42.4 10.6 %all-to-all-start = ((bf16[16,4,1,4,2048]{4,3,1,2,0:T(4,128)(2,1)}), bf16[16,4,1,4,2048]{4,3,1,2,0:T(4,128)(2,1)S(1)}, u32[]{:S(2)}, u32[]{:S(2)}) async-start(bf16[16,4,1,4,2048]{4,3,1,2,0:T(4,128)(2,1)} %fusion.28), calls=%async_computation | async-start | bytes 2097152 | tf_op jit(solution)/shard_map/all_to_all | solution.py:118
  54.5 26.6 %all-to-all-done = bf16[16,4,1,4,2048]{4,3,1,2,0:T(4,128)(2,1)S(1)} async-done(((bf16[16,4,1,4,2048]{4,3,1,2,0:T(4,128)(2,1)}), bf16[16,4,1,4,2048]{4,3,1,2,0:T(4,128)(2,1)S(1)}, u32[]{:S(2)}, u32[]{:S(2)}) %all-to-all-start) | async-done | bytes 1048608 | tf_op jit(solution)/shard_map/all_to_all | solution.py:118
  83.9 3.0 %copy.543 = bf16[8,16,4,2048]{3,2,1,0:T(4,128)(2,1)} copy(bf16[8,16,4,2048]{3,1,2,0:T(8,128)(2,1)S(1)} %pad_maximum_fusion.2) | data formatting | bytes 4194304 | tf_op jit(solution)/shard_map/concatenate | solution.py:55
  86.8 4.0 %convert_element_type.68 = bf16[512,2048]{1,0:T(8,128)(2,1)} reshape(bf16[8,16,4,2048]{3,2,1,0:T(4,128)(2,1)} %copy.543) | data formatting | bytes 4194304 | tf_op jit(solution)/shard_map/convert_element_type | solution.py:55
  90.8 7.6 %fusion.80 = f32[512,2048]{1,0:T(8,128)S(1)} fusion(bf16[512,2048]{1,0:T(8,128)(2,1)} %convert_element_type.68, bf16[2048,2048]{1,0:T(8,128)(2,1)} %param.9), kind=kOutput, calls=%fused_computation.118 | convolution fusion | flops 4294967296 | bytes 14680064 | tf_op jit(solution)/shard_map/dot_general | solution.py:57
  98.4 2.3 %fusion.77 = (f32[256,2048]{1,0:T(8,128)}, f32[256,2048]{1,0:T(8,128)}) fusion(f32[512,2048]{1,0:T(8,128)S(1)} %fusion.80), kind=kLoop, calls=%fused_computation.115 | loop fusion | bytes 8388608 | tf_op jit(solution)/shard_map/slice | solution.py:66
  100.7 2.9 %squeeze.14 = f32[4,16,4,2048]{3,2,1,0:T(4,128)} reshape(f32[256,2048]{1,0:T(8,128)} %get-tuple-element.8) | data formatting | bytes 4194304 | tf_op jit(solution)/shard_map/squeeze | solution.py:66
  103.5 2.9 %squeeze.15 = f32[4,16,4,2048]{3,2,1,0:T(4,128)} reshape(f32[256,2048]{1,0:T(8,128)} %get-tuple-element.7) | data formatting | bytes 4194304 | tf_op jit(solution)/shard_map/squeeze | solution.py:66
  106.5 3.3 %fusion.18 = (bf16[4,16,4,2048]{3,2,1,0:T(4,128)(2,1)S(1)}, bf16[4,16,4,2048]{3,2,1,0:T(4,128)(2,1)S(1)}) fusion(f32[4,16,4,2048]{3,2,1,0:T(4,128)} %squeeze.15, f32[4,16,4,2048]{3,2,1,0:T(4,128)} %squeeze.14, f32[4,16,2048]{2,1,0:T(8,128)S(1)} %copy-done.2, f32[16]{0:T(128)S(1)} %sine_multiply_fusion, f32[4,16,2048]{2,1,0:T(8,128)S(1)} %copy-done.1), kind=kLoop, calls=%fused_computation.31 | loop fusion | flops 5242880 | bytes 7340096 | tf_op jit(solution)/shard_map/convert
  109.8 2.7 %pad_maximum_fusion.3 = bf16[8,16,4,2048]{3,2,1,0:T(4,128)(2,1)} fusion(bf16[4,16,4,2048]{3,2,1,0:T(4,128)(2,1)S(1)} %get-tuple-element.6, bf16[4,16,4,2048]{3,2,1,0:T(4,128)(2,1)S(1)} %get-tuple-element.5), kind=kLoop, calls=%fused_computation.26 | loop fusion | flops 1048576 | bytes 4194304 | tf_op jit(solution)/shard_map/concatenate | solution.py:69
  112.5 4.0 %convert_element_type.70 = bf16[512,2048]{1,0:T(8,128)(2,1)} reshape(bf16[8,16,4,2048]{3,2,1,0:T(4,128)(2,1)} %pad_maximum_fusion.3) | data formatting | bytes 4194304 | tf_op jit(solution)/shard_map/convert_element_type | solution.py:70
  116.4 8.5 %convolution_convert_fusion = bf16[512,2048]{1,0:T(8,128)(2,1)S(1)} fusion(bf16[512,2048]{1,0:T(8,128)(2,1)} %convert_element_type.70, bf16[2048,2048]{1,0:T(8,128)(2,1)} %param.9), kind=kOutput, calls=%fused_computation | convolution fusion | flops 4296015872 | bytes 12582912 | tf_op jit(solution)/shard_map/dot_general | solution.py:44
  127.9 2.7 %fusion.23 = f32[4,4,2048,16]{2,3,1,0:T(8,128)} fusion(bf16[4,16,4,2048]{3,2,1,0:T(4,128)(2,1)S(1)} %squeeze.16), kind=kOutput, calls=%fused_computation.36 | convolution fusion | flops 100666880 | bytes 3145728 | tf_op jit(solution)/shard_map/kn,fnrx->fkrx/dot_general | solution.py:38
  132.0 3.1 %fusion.1 = f32[4,16,4,2048]{3,1,2,0:T(8,128)S(1)} fusion(f32[4,4,2048,16]{2,3,1,0:T(8,128)} %fusion.23, bf16[4,16,4,2048]{3,2,1,0:T(4,128)(2,1)S(1)} %squeeze.17), kind=kOutput, calls=%fused_computation.5 | convolution fusion | flops 101715456 | bytes 5242880 | tf_op jit(solution)/shard_map/kn,fnrx->fkrx/dot_general | solution.py:38
  135.1 2.7 %copy.546 = f32[4,16,4,2048]{3,2,0,1:T(4,128)} copy(f32[4,16,4,2048]{3,1,2,0:T(8,128)S(1)} %fusion.1) | data formatting | bytes 4194304 | tf_op jit(solution)/shard_map/div | solution.py:128
  137.8 4.6 %all-to-all-start.1 = ((f32[4,16,4,2048]{3,2,0,1:T(4,128)}), f32[4,16,4,2048]{3,2,0,1:T(4,128)}, u32[]{:S(2)}, u32[]{:S(2)}) async-start(f32[4,16,4,2048]{3,2,0,1:T(4,128)} %copy.546), calls=%async_computation.1 | async-start | bytes 4194304 | tf_op jit(solution)/shard_map/all_to_all | solution.py:131
  142.4 47.9 %all-to-all-done.1 = f32[4,16,4,2048]{3,2,0,1:T(4,128)} async-done(((f32[4,16,4,2048]{3,2,0,1:T(4,128)}), f32[4,16,4,2048]{3,2,0,1:T(4,128)}, u32[]{:S(2)}, u32[]{:S(2)}) %all-to-all-start.1) | async-done | bytes 2097184 | tf_op jit(solution)/shard_map/all_to_all | solution.py:131
  190.3 2.8 %copy_multiply_fusion = f32[4,16,4,2048]{3,1,2,0:T(8,128)S(1)} fusion(f32[4,16,4,2048]{3,2,0,1:T(4,128)} %all-to-all-done.1, f32[]{:T(128)S(6)} %pow.8), kind=kLoop, calls=%fused_computation.28 | loop fusion | flops 524288 | bytes 4194308 | tf_op jit(solution)/shard_map/mul | solution.py:132
  194.5 2.6 %copy_add_fusion = f32[4,1,64,2048]{3,2,1,0:T(8,128)} fusion(f32[4,1,64,2048]{3,2,1,0:T(8,128)S(1)} %copy-done, f32[4,1,64,2048]{3,0,2,1:T(4,128)S(1)} %bitcast.103), kind=kLoop, calls=%fused_computation.27 | loop fusion | flops 524288 | bytes 6291456 | tf_op jit(solution)/shard_map/add | solution.py:132
  (50 shorter events, 24.8 us)
Async XLA Ops:
  0.0 14.2 %copy-start.3 = (s32[64,2048]{1,0:T(8,128)S(1)}, s32[64,2048]{1,0:T(8,128)}, u32[]{:S(2)}) copy-start(s32[64,2048]{1,0:T(8,128)} %param.13) | copy-start | bytes 1572868
  0.0 28.3 %collective-permute-start.2 = (f32[4,1,64,2048]{3,2,1,0:T(8,128)}, f32[4,1,64,2048]{3,2,1,0:T(8,128)}, u32[]{:S(2)}, u32[]{:S(2)}) collective-permute-start(f32[4,1,64,2048]{3,2,1,0:T(8,128)} %param.7), channel_id=1, source_target_pairs={{0,16},{16,32},{32,48},{48,64},{64,80},{80,96},{96,112},{112,128},... | collective-permute-start | bytes 6291464 | tf_op jit(solution)/shard_map/ppermute | solution.py:28
  6.1 20.4 %collective-permute-start = (f32[4,1,1,2048]{3,2,1,0:T(1,128)S(1)}, f32[4,1,1,2048]{3,2,1,0:T(1,128)S(1)}, u32[]{:S(2)}, u32[]{:S(2)}) collective-permute-start(f32[4,1,1,2048]{3,2,1,0:T(1,128)S(1)} %get-tuple-element.11), channel_id=1, source_target_pairs={{1,0},{2,1},{3,2},{4,3},{5,4},{6,5},{7,6},{8,7},{9,8},{10,9},{11,1... | collective-permute-start | bytes 98312 | tf_op jit(solution)/shard_map/ppermute | solution.py:20
  7.4 6.8 %copy-start.4 = (f32[2048]{0:T(1024)S(1)}, f32[2048]{0:T(1024)}, u32[]{:S(2)}) copy-start(f32[2048]{0:T(1024)} %param.10) | copy-start | bytes 24580
  7.5 19.1 %collective-permute-start.1 = (f32[4,1,1,2048]{3,2,1,0:T(1,128)S(1)}, f32[4,1,1,2048]{3,2,1,0:T(1,128)S(1)}, u32[]{:S(2)}, u32[]{:S(2)}) collective-permute-start(f32[4,1,1,2048]{3,2,1,0:T(1,128)S(1)} %get-tuple-element.12), channel_id=1, source_target_pairs={{0,1},{1,2},{2,3},{3,4},{4,5},{5,6},{6,7},{7,8},{8,9},{9,10},{10,1... | collective-permute-start | bytes 98312 | tf_op jit(solution)/shard_map/ppermute | solution.py:17
  14.2 12.1 %copy-start.5 = (f32[8]{0:T(128)S(1)}, f32[8]{0:T(128)}, u32[]{:S(2)}) copy-start(f32[8]{0:T(128)} %param.11) | copy-start | bytes 100
  14.2 12.1 %copy-start.6 = (s32[4]{0:T(128)S(1)}, s32[4]{0:T(128)}, u32[]{:S(2)}) copy-start(s32[4]{0:T(128)} %param.12) | copy-start | bytes 52
  14.2 14.1 %copy-start = (f32[4,1,64,2048]{3,2,1,0:T(8,128)S(1)}, f32[4,1,64,2048]{3,2,1,0:T(8,128)}, u32[]{:S(2)}) copy-start(f32[4,1,64,2048]{3,2,1,0:T(8,128)} %param.7) | copy-start | bytes 6291460
  42.4 38.6 %all-to-all-start = ((bf16[16,4,1,4,2048]{4,3,1,2,0:T(4,128)(2,1)}), bf16[16,4,1,4,2048]{4,3,1,2,0:T(4,128)(2,1)S(1)}, u32[]{:S(2)}, u32[]{:S(2)}) async-start(bf16[16,4,1,4,2048]{4,3,1,2,0:T(4,128)(2,1)} %fusion.28), calls=%async_computation | async-start | bytes 2097152 | tf_op jit(solution)/shard_map/all_to_all | solution.py:118
  103.5 3.0 %copy-start.1 = (f32[4,16,2048]{2,1,0:T(8,128)S(1)}, f32[4,16,2048]{2,1,0:T(8,128)}, u32[]{:S(2)}) copy-start(f32[4,16,2048]{2,1,0:T(8,128)} %get-tuple-element.13) | copy-start | bytes 1572868
  103.5 3.0 %copy-start.2 = (f32[4,16,2048]{2,1,0:T(8,128)S(1)}, f32[4,16,2048]{2,1,0:T(8,128)}, u32[]{:S(2)}) copy-start(f32[4,16,2048]{2,1,0:T(8,128)} %get-tuple-element.14) | copy-start | bytes 1572868
  137.8 52.5 %all-to-all-start.1 = ((f32[4,16,4,2048]{3,2,0,1:T(4,128)}), f32[4,16,4,2048]{3,2,0,1:T(4,128)}, u32[]{:S(2)}, u32[]{:S(2)}) async-start(f32[4,16,4,2048]{3,2,0,1:T(4,128)} %copy.546), calls=%async_computation.1 | async-start | bytes 4194304 | tf_op jit(solution)/shard_map/all_to_all | solution.py:131
